TPU v7x, 512 devices: a whole 4x4x16 slice. The times are simulated.
512 devices in a mesh: blk: 4 (over y), uly: 32 (over z, x_hi), dp: 4 (over x_lo, core).
Axes of the slice: x: 4 (x_hi: 2, x_lo: 2; x = x_hi * 2 + x_lo), y: 4, z: 16, core: 2. Of those that a mesh axis runs over, the one named last changes fastest.
Arguments:
- queries: bfloat16 [4, 16384, 4096], P(None, ('blk', 'uly', 'dp')), may hold values from -16 to 16
- keys: bfloat16 [4, 16384, 512], P(None, ('blk', 'uly', 'dp')), may hold values from -16 to 16
- values: bfloat16 [4, 16384, 512], P(None, ('blk', 'uly', 'dp')), may hold values from -6 to 6
- grad_out: bfloat16 [4, 16384, 4096], P(None, ('blk', 'uly', 'dp')), may hold values from -6 to 6
- segment_ids: int32 [4, 16384], replicated, may hold values from 0 to 63, never falling along the last dimension, each value on 1 to 512 neighbouring positions
- assignment: int32 [4], replicated, may hold values from 0 to 3, each once
Outputs:
- grad_queries: bfloat16 [4, 16384, 32, 128], P('dp', ('blk', 'uly'))
- grad_keys: bfloat16 [4, 16384, 512], P('dp', ('blk', 'uly'))
- grad_values: bfloat16 [4, 16384, 512], P('dp', ('blk', 'uly'))
Inputs may be any that keep to these rules, and one draw needn't show every extreme that they name: `segment_ids`: no document holds more than 512 tokens, and some document holds exactly 512.
All inputs are finite; a program needn't handle non-finite values.
Results may differ from a plain program's by a relative error of at most 0.008.
Values may be sent and summed in bfloat16 or wider, within the bound.
A program may use at most 64 MiB of HBM per device.

v0:
```python
import jax
import jax.numpy as jnp
from jax import lax
from jax.sharding import PartitionSpec as P

QH = 32
KVH = 4
HD = 128


def shifted(value, axis, by):
    length = lax.axis_size(axis)
    pairs = [(i, i + by) for i in range(length) if 0 <= i + by < length]
    return lax.ppermute(value, axis, pairs)


def attend(query_four, grad_four, key_pad, value_pad, segment_pad, block_rows, rim_rows):
    total_rows = query_four.shape[0]
    head_ratio = query_four.shape[2]
    nblocks = total_rows // block_rows
    softmax_scale = 1.0 / HD**0.5
    row_pos = jnp.arange(block_rows, dtype=jnp.int32) + rim_rows
    col_pos = jnp.arange(rim_rows + block_rows, dtype=jnp.int32)
    query_heads = query_four.transpose(1, 0, 2, 3)
    grad_heads = grad_four.transpose(1, 0, 2, 3)
    key_heads = key_pad.transpose(1, 0, 2)
    value_heads = value_pad.transpose(1, 0, 2)

    def one_head(items):
        query_three, grad_three, key_two, value_two = items

        def block_step(carry, index):
            key_acc, value_acc = carry
            start = index * block_rows
            query_block = lax.dynamic_slice_in_dim(query_three, start, block_rows, 0)
            grad_block = lax.dynamic_slice_in_dim(grad_three, start, block_rows, 0)
            key_window = lax.dynamic_slice_in_dim(key_two, start, rim_rows + block_rows, 0)
            value_window = lax.dynamic_slice_in_dim(value_two, start, rim_rows + block_rows, 0)
            segment_query = lax.dynamic_slice_in_dim(segment_pad, start + rim_rows, block_rows, 0)
            segment_key = lax.dynamic_slice_in_dim(segment_pad, start, rim_rows + block_rows, 0)
            allowed = (segment_query[:, None] == segment_key[None, :]) & (
                col_pos[None, :] <= row_pos[:, None]
            )
            scores = (
                jnp.einsum(
                    "qrd,kd->rqk", query_block, key_window, preferred_element_type=jnp.float32
                )
                * softmax_scale
            )
            scores = jnp.where(allowed, scores, -jnp.inf)
            top_score = jnp.max(scores, axis=-1, keepdims=True)
            weights = jnp.where(allowed, jnp.exp(scores - top_score), 0.0)
            probs = weights / jnp.sum(weights, axis=-1, keepdims=True)
            probs_half = probs.astype(jnp.bfloat16)
            grad_value = jnp.einsum(
                "rqk,qrd->kd", probs_half, grad_block, preferred_element_type=jnp.float32
            )
            grad_probs = jnp.einsum(
                "qrd,kd->rqk", grad_block, value_window, preferred_element_type=jnp.float32
            )
            row_delta = jnp.sum(probs * grad_probs, axis=-1, keepdims=True)
            grad_scores = (softmax_scale * probs * (grad_probs - row_delta)).astype(jnp.bfloat16)
            grad_query = jnp.einsum(
                "rqk,kd->qrd", grad_scores, key_window, preferred_element_type=jnp.float32
            ).astype(jnp.bfloat16)
            grad_key = jnp.einsum(
                "rqk,qrd->kd", grad_scores, query_block, preferred_element_type=jnp.float32
            )
            old_key = lax.dynamic_slice_in_dim(key_acc, start, rim_rows + block_rows, 0)
            old_value = lax.dynamic_slice_in_dim(value_acc, start, rim_rows + block_rows, 0)
            key_acc = lax.dynamic_update_slice_in_dim(key_acc, old_key + grad_key, start, 0)
            value_acc = lax.dynamic_update_slice_in_dim(value_acc, old_value + grad_value, start, 0)
            return ((key_acc, value_acc), grad_query)

        start_acc = jnp.zeros((rim_rows + total_rows, HD), jnp.float32)
        (key_acc, value_acc), grad_blocks = lax.scan(
            block_step, (start_acc, start_acc), jnp.arange(nblocks, dtype=jnp.int32)
        )
        return (grad_blocks.reshape(total_rows, head_ratio, HD), key_acc, value_acc)

    grad_query, key_acc, value_acc = lax.map(
        one_head, (query_heads, grad_heads, key_heads, value_heads)
    )
    local_kv = query_four.shape[1]
    grad_query = grad_query.transpose(1, 0, 2, 3).reshape(total_rows, local_kv * head_ratio, HD)
    return (grad_query, key_acc.transpose(1, 0, 2), value_acc.transpose(1, 0, 2))


def shards(queries, keys, values, grad_out, segment_ids, assignment):
    n_heads_axis = lax.axis_size("uly")
    group_index = lax.axis_index("dp")
    blk_index = lax.axis_index("blk")
    query_pick = jnp.take(queries, assignment, axis=0)
    key_pick = jnp.take(keys, assignment, axis=0)
    value_pick = jnp.take(values, assignment, axis=0)
    grad_pick = jnp.take(grad_out, assignment, axis=0)
    query_tok, key_tok, value_tok, grad_tok = (
        lax.all_to_all(query_pick, "dp", split_axis=0, concat_axis=1, tiled=True),
        lax.all_to_all(key_pick, "dp", split_axis=0, concat_axis=1, tiled=True),
        lax.all_to_all(value_pick, "dp", split_axis=0, concat_axis=1, tiled=True),
        lax.all_to_all(grad_pick, "dp", split_axis=0, concat_axis=1, tiled=True),
    )
    tok_dev = query_tok.shape[1]
    query_tok = query_tok.reshape(tok_dev, QH, HD)
    grad_tok = grad_tok.reshape(tok_dev, QH, HD)
    key_tok = key_tok.reshape(tok_dev, KVH, HD)
    value_tok = value_tok.reshape(tok_dev, KVH, HD)
    segment_row = jnp.take(segment_ids, assignment[group_index], axis=0)
    copies = max(1, n_heads_axis // KVH)
    key_rep = jnp.repeat(key_tok, copies, axis=1)
    value_rep = jnp.repeat(value_tok, copies, axis=1)
    query_local, grad_local, key_local, value_local = (
        lax.all_to_all(query_tok, "uly", split_axis=1, concat_axis=0, tiled=True),
        lax.all_to_all(grad_tok, "uly", split_axis=1, concat_axis=0, tiled=True),
        lax.all_to_all(key_rep, "uly", split_axis=1, concat_axis=0, tiled=True),
        lax.all_to_all(value_rep, "uly", split_axis=1, concat_axis=0, tiled=True),
    )
    range_tok = query_local.shape[0]
    local_query = query_local.shape[1]
    local_kv = key_local.shape[1]
    head_ratio = local_query // local_kv
    block_rows = min(512, range_tok)
    rim_key, rim_value = shifted(
        (key_local[range_tok - block_rows :], value_local[range_tok - block_rows :]), "blk", 1
    )
    key_pad = jnp.concatenate([rim_key, key_local], axis=0)
    value_pad = jnp.concatenate([rim_value, value_local], axis=0)
    range_start = blk_index * range_tok
    segment_own = lax.dynamic_slice_in_dim(segment_row, range_start, range_tok, 0)
    segment_prev = lax.dynamic_slice_in_dim(
        segment_row, jnp.maximum(range_start - block_rows, 0), block_rows, 0
    )
    segment_prev = jnp.where(blk_index > 0, segment_prev, -1)
    segment_pad = jnp.concatenate([segment_prev, segment_own], axis=0)
    query_four = query_local.reshape(range_tok, local_kv, head_ratio, HD)
    grad_four = grad_local.reshape(range_tok, local_kv, head_ratio, HD)
    grad_query, key_acc, value_acc = attend(
        query_four, grad_four, key_pad, value_pad, segment_pad, block_rows, block_rows
    )
    back_key, back_value = (
        shifted(key_acc[:block_rows].astype(jnp.bfloat16), "blk", -1).astype(jnp.float32),
        shifted(value_acc[:block_rows].astype(jnp.bfloat16), "blk", -1).astype(jnp.float32),
    )
    key_own = key_acc[block_rows:].at[range_tok - block_rows :].add(back_key)
    value_own = value_acc[block_rows:].at[range_tok - block_rows :].add(back_value)
    key_home, value_home = (
        lax.all_to_all(
            key_own.astype(jnp.bfloat16), "uly", split_axis=0, concat_axis=1, tiled=True
        ).astype(key_own.dtype),
        lax.all_to_all(
            value_own.astype(jnp.bfloat16), "uly", split_axis=0, concat_axis=1, tiled=True
        ).astype(value_own.dtype),
    )
    grad_keys = (
        key_home.reshape(tok_dev, KVH, copies, HD)
        .sum(axis=2)
        .astype(jnp.bfloat16)
        .reshape(1, tok_dev, KVH * HD)
    )
    grad_values = (
        value_home.reshape(tok_dev, KVH, copies, HD)
        .sum(axis=2)
        .astype(jnp.bfloat16)
        .reshape(1, tok_dev, KVH * HD)
    )
    query_home = lax.all_to_all(grad_query, "uly", split_axis=0, concat_axis=1, tiled=True)
    grad_queries = query_home.reshape(1, tok_dev, QH, HD)
    return (grad_queries, grad_keys, grad_values)


def solution(mesh):
    in_specs = (
        P(None, ("blk", "uly", "dp"), None),
        P(None, ("blk", "uly", "dp"), None),
        P(None, ("blk", "uly", "dp"), None),
        P(None, ("blk", "uly", "dp"), None),
        P(),
        P(),
    )
    out_specs = (
        P("dp", ("blk", "uly"), None, None),
        P("dp", ("blk", "uly"), None),
        P("dp", ("blk", "uly"), None),
    )
    return jax.shard_map(shards, mesh=mesh, in_specs=in_specs, out_specs=out_specs, check_vma=False)
```

profile of v0, /device:TPU:52, one launch (start us, length us, event | category | flops | bytes accessed | tf_op | source)
XLA Modules:
  0.0 637.3 jit_solution(9994790855314164120)
XLA Ops:
  5.8 3.3 all-to-all-start
  9.8 1.8 gather_fusion.3
  11.6 2.1 all-to-all-done
  13.7 3.3 all-to-all-start.4
  18.6 3.0 all-to-all-done.4
  21.6 18.8 %all_to_all.135 = bf16[4,32,4096]{2,1,0:T(8,128)(2,1)} all-to-all(bf16[4,32,4096]{2,1,0:T(8,128)(2,1)} %get-tuple-element.287), channel_id=1, replica_groups=mesh['blk'=4,'uly'=32,'dp'=4] {'dp'}, dimensions={0} | all-to-all | bytes 2097152 | tf_op jit(solution)/shard_map/all_to_all | solution.py:98
  40.3 3.5 all-to-all-start.6
  43.9 14.3 %all-to-all-done.6 = bf16[4,32,4096]{2,1,0:T(8,128)(2,1)S(1)} async-done(((bf16[4,32,4096]{2,1,0:T(8,128)(2,1)}), bf16[4,32,4096]{2,1,0:T(8,128)(2,1)S(1)}, u32[]{:S(2)}, u32[]{:S(2)}) %all-to-all-start.6) | async-done | bytes 1048608 | tf_op jit(solution)/shard_map/all_to_all | solution.py:101
  59.6 17.8 %all-to-all-start.1 = ((bf16[128,32,128]{2,0,1:T(8,128)(2,1)}), bf16[128,32,128]{2,0,1:T(8,128)(2,1)S(1)}, u32[]{:S(2)}, u32[]{:S(2)}) async-start(bf16[128,32,128]{2,0,1:T(8,128)(2,1)} %bitcast.3), calls=%async_computation.1 | async-start | bytes 2097152 | tf_op jit(solution)/shard_map/all_to_all | solution.py:115
  77.4 53.9 %all-to-all-done.1 = bf16[128,32,128]{2,0,1:T(8,128)(2,1)S(1)} async-done(((bf16[128,32,128]{2,0,1:T(8,128)(2,1)}), bf16[128,32,128]{2,0,1:T(8,128)(2,1)S(1)}, u32[]{:S(2)}, u32[]{:S(2)}) %all-to-all-start.1) | async-done | bytes 1048608 | tf_op jit(solution)/shard_map/all_to_all | solution.py:115
  132.6 6.1 all-to-all-start.5
  141.5 51.2 %all-to-all-done.5 = bf16[128,32,128]{2,0,1:T(8,128)(2,1)S(1)} async-done(((bf16[128,32,128]{2,0,1:T(8,128)(2,1)}), bf16[128,32,128]{2,0,1:T(8,128)(2,1)S(1)}, u32[]{:S(2)}, u32[]{:S(2)}) %all-to-all-start.5) | async-done | bytes 1048608 | tf_op jit(solution)/shard_map/all_to_all | solution.py:116
  192.7 6.2 all-to-all-start.3
  201.7 51.2 %all-to-all-done.3 = bf16[128,32,128]{2,0,1:T(8,128)(2,1)} async-done(((bf16[128,32,128]{2,0,1:T(8,128)(2,1)}), bf16[128,32,128]{2,0,1:T(8,128)(2,1)}, u32[]{:S(2)}, u32[]{:S(2)}) %all-to-all-start.3) | async-done | bytes 1048608 | tf_op jit(solution)/shard_map/all_to_all | solution.py:113
  252.9 6.2 all-to-all-start.7
  262.7 3.2 collective-permute-start
  266.6 1.9 collective-permute-start.1
  270.7 2.8 collective-permute-done.1
  274.6 38.6 %all-to-all-done.7 = bf16[128,32,128]{2,0,1:T(8,128)(2,1)} async-done(((bf16[128,32,128]{2,0,1:T(8,128)(2,1)}), bf16[128,32,128]{2,0,1:T(8,128)(2,1)}, u32[]{:S(2)}, u32[]{:S(2)}) %all-to-all-start.7) | async-done | bytes 1048608 | tf_op jit(solution)/shard_map/all_to_all | solution.py:114
  314.9 127.9 %while.31 = (s32[]{:T(128)}, f32[4608,128]{1,0:T(8,128)S(1)}, f32[4608,128]{1,0:T(8,128)}, bf16[8,512,1,128]{3,1,0,2:T(8,128)(2,1)}, s32[8]{0:T(128)S(1)}, /*ind...) while((s32[]{:T(128)}, f32[4608,128]{1,0:T(8,128)S(1)}, ...), condition=%wide.region_4.7_spmd.clone, body=%wide.region_0.6_spmd.clone.sunk | while | flops 695008256 | bytes 21967688 | solution.py:76
  320.0 3.0 fusion.67
  323.0 1.9 fusion.64
  327.3 2.0 fusion.68
  336.0 3.0 fusion.67
  339.0 1.9 fusion.64
  343.2 2.0 fusion.68
  352.0 3.0 fusion.67
  355.0 1.9 fusion.64
  359.2 2.0 fusion.68
  368.0 3.0 fusion.67
  371.0 1.9 fusion.64
  375.2 2.0 fusion.68
  384.0 3.0 fusion.67
  387.0 1.9 fusion.64
  391.2 2.0 fusion.68
  400.0 3.0 fusion.67
  403.0 1.9 fusion.64
  407.2 2.0 fusion.68
  416.0 3.0 fusion.67
  419.0 1.9 fusion.64
  423.2 2.0 fusion.68
  432.0 3.0 fusion.67
  435.0 1.9 fusion.64
  439.2 2.0 fusion.68
  443.4 3.3 reduce.18
  446.7 2.1 reshape.435
  448.8 6.2 all-to-all-start.8
  456.0 2.5 collective-permute-start.3
  460.2 2.6 collective-permute-done.3
  463.9 2.7 convert_element_type.109
  466.6 24.4 %reduce.20 = bf16[4096,128]{1,0:T(8,128)(2,1)} reduce(bf16[4096,1,128]{2,1,0:T(2,128)(2,1)} %convert_element_type.109, bf16[]{:T(256)} %broadcast.248), dimensions={1}, to_apply=%convert_element_type.109.reduce_sub_computation | reduce | bytes 2097154 | tf_op jit(solution)/shard_map/convert_element_type | solution.py:151
  491.0 2.2 reshape.439
  493.2 15.9 %all-to-all-done.8 = bf16[32,2,8192]{2,1,0:T(2,128)(2,1)} async-done(((bf16[32,2,8192]{2,1,0:T(2,128)(2,1)}), bf16[32,2,8192]{2,1,0:T(2,128)(2,1)}, u32[]{:S(2)}, u32[]{:S(2)}) %all-to-all-start.8) | async-done | bytes 1048608 | tf_op jit(solution)/shard_map/all_to_all | solution.py:166
  509.1 6.2 all-to-all-start.10
  515.3 2.4 collective-permute-start.2
  517.8 4.4 collective-permute-done.2
  523.7 23.4 %reduce.19 = bf16[4096,128]{1,0:T(8,128)(2,1)} reduce(bf16[4096,1,128]{2,1,0:T(2,128)(2,1)S(1)} %convert_element_type.101, bf16[]{:T(256)} %broadcast.248), dimensions={1}, to_apply=%convert_element_type.101.reduce_sub_computation | reduce | bytes 2097154 | tf_op jit(solution)/shard_map/convert_element_type | solution.py:148
  547.1 2.1 reshape.437
  549.2 20.1 %all-to-all-done.10 = bf16[32,2,8192]{2,1,0:T(2,128)(2,1)} async-done(((bf16[32,2,8192]{2,1,0:T(2,128)(2,1)}), bf16[32,2,8192]{2,1,0:T(2,128)(2,1)}, u32[]{:S(2)}, u32[]{:S(2)}) %all-to-all-start.10) | async-done | bytes 1048608 | tf_op jit(solution)/shard_map/all_to_all | solution.py:150
  569.3 6.2 all-to-all-start.9
  575.5 4.3 reshape.436
  581.6 4.3 reshape.440
  589.3 40.3 %all-to-all-done.9 = bf16[32,2,8192]{2,1,0:T(2,128)(2,1)} async-done(((bf16[32,2,8192]{2,1,0:T(2,128)(2,1)}), bf16[32,2,8192]{2,1,0:T(2,128)(2,1)}, u32[]{:S(2)}, u32[]{:S(2)}) %all-to-all-start.9) | async-done | bytes 1048608 | tf_op jit(solution)/shard_map/all_to_all | solution.py:147
  629.6 4.3 reshape.438
  (138 shorter events, 105.1 us)
Async XLA Ops:
  0.6 8.5 %copy-start = (bf16[4,32,4096]{2,1,0:T(8,128)(2,1)S(1)}, bf16[4,32,4096]{2,1,0:T(8,128)(2,1)}, u32[]{:S(2)}) copy-start(bf16[4,32,4096]{2,1,0:T(8,128)(2,1)} %param.16) | copy-start | bytes 3145732
  5.8 7.9 %all-to-all-start = ((bf16[4,32,512]{2,1,0:T(8,128)(2,1)}), bf16[4,32,512]{2,1,0:T(8,128)(2,1)S(1)}, u32[]{:S(2)}, u32[]{:S(2)}) async-start(bf16[4,32,512]{2,1,0:T(8,128)(2,1)} %get-tuple-element.289), calls=%async_computation | async-start | bytes 262144 | tf_op jit(solution)/shard_map/all_to_all | solution.py:99
  13.7 7.9 %all-to-all-start.4 = ((bf16[4,32,512]{2,1,0:T(8,128)(2,1)}), bf16[4,32,512]{2,1,0:T(8,128)(2,1)S(1)}, u32[]{:S(2)}, u32[]{:S(2)}) async-start(bf16[4,32,512]{2,1,0:T(8,128)(2,1)} %get-tuple-element.288), calls=%async_computation.4 | async-start | bytes 262144 | tf_op jit(solution)/shard_map/all_to_all | solution.py:100
  40.3 17.9 %all-to-all-start.6 = ((bf16[4,32,4096]{2,1,0:T(8,128)(2,1)}), bf16[4,32,4096]{2,1,0:T(8,128)(2,1)S(1)}, u32[]{:S(2)}, u32[]{:S(2)}) async-start(bf16[4,32,4096]{2,1,0:T(8,128)(2,1)} %get-tuple-element.286), calls=%async_computation.6 | async-start | bytes 2097152 | tf_op jit(solution)/shard_map/all_to_all | solution.py:101
  58.3 1.3 copy-start.1
  59.6 71.8 %all-to-all-start.1 = ((bf16[128,32,128]{2,0,1:T(8,128)(2,1)}), bf16[128,32,128]{2,0,1:T(8,128)(2,1)S(1)}, u32[]{:S(2)}, u32[]{:S(2)}) async-start(bf16[128,32,128]{2,0,1:T(8,128)(2,1)} %bitcast.3), calls=%async_computation.1 | async-start | bytes 2097152 | tf_op jit(solution)/shard_map/all_to_all | solution.py:115
  132.6 60.1 %all-to-all-start.5 = ((bf16[128,32,128]{2,0,1:T(8,128)(2,1)}), bf16[128,32,128]{2,0,1:T(8,128)(2,1)S(1)}, u32[]{:S(2)}, u32[]{:S(2)}) async-start(bf16[128,32,128]{2,0,1:T(8,128)(2,1)} %bitcast.174), calls=%async_computation.5 | async-start | bytes 2097152 | tf_op jit(solution)/shard_map/all_to_all | solution.py:116
  192.7 60.3 %all-to-all-start.3 = ((bf16[128,32,128]{2,0,1:T(8,128)(2,1)}), bf16[128,32,128]{2,0,1:T(8,128)(2,1)}, u32[]{:S(2)}, u32[]{:S(2)}) async-start(bf16[128,32,128]{2,0,1:T(8,128)(2,1)} %copy.31), calls=%async_computation.3 | async-start | bytes 2097152 | tf_op jit(solution)/shard_map/all_to_all | solution.py:113
  200.3 58.8 %copy-start.2 = (s32[4]{0:T(128)S(1)}, s32[4]{0:T(128)}, u32[]{:S(2)}) copy-start(s32[4]{0:T(128)} %param.21) | copy-start | bytes 52
  252.9 60.2 %all-to-all-start.7 = ((bf16[128,32,128]{2,0,1:T(8,128)(2,1)}), bf16[128,32,128]{2,0,1:T(8,128)(2,1)}, u32[]{:S(2)}, u32[]{:S(2)}) async-start(bf16[128,32,128]{2,0,1:T(8,128)(2,1)} %copy.33), calls=%async_computation.7 | async-start | bytes 2097152 | tf_op jit(solution)/shard_map/all_to_all | solution.py:114
  262.7 6.9 %collective-permute-start = (bf16[512,1,128]{2,0,1:T(8,128)(2,1)S(1)}, bf16[512,1,128]{2,0,1:T(8,128)(2,1)S(1)}, u32[]{:S(2)}, u32[]{:S(2)}) collective-permute-start(bf16[512,1,128]{2,0,1:T(8,128)(2,1)S(1)} %bitcast.182), channel_id=1, source_target_pairs={{0,128},{128,256},{256,384},{1,129},{129,257},{257,385},{2,130},{1... | collective-permute-start | bytes 393224 | tf_op jit(solution)/shard_map/ppermute | solution.py:14
  266.6 6.9 %collective-permute-start.1 = (bf16[512,1,128]{2,0,1:T(8,128)(2,1)S(1)}, bf16[512,1,128]{2,0,1:T(8,128)(2,1)S(1)}, u32[]{:S(2)}, u32[]{:S(2)}) collective-permute-start(bf16[512,1,128]{2,0,1:T(8,128)(2,1)S(1)} %bitcast.183), channel_id=1, source_target_pairs={{0,128},{128,256},{256,384},{1,129},{129,257},{257,385},{2,130},{1... | collective-permute-start | bytes 393224 | tf_op jit(solution)/shard_map/ppermute | solution.py:14
  448.8 60.2 %all-to-all-start.8 = ((bf16[32,2,8192]{2,1,0:T(2,128)(2,1)}), bf16[32,2,8192]{2,1,0:T(2,128)(2,1)}, u32[]{:S(2)}, u32[]{:S(2)}) async-start(bf16[32,2,8192]{2,1,0:T(2,128)(2,1)} %reshape.435), calls=%async_computation.8 | async-start | bytes 2097152 | tf_op jit(solution)/shard_map/all_to_all | solution.py:166
  456.0 6.9 %collective-permute-start.3 = (bf16[512,1,128]{2,0,1:T(8,128)(2,1)S(1)}, bf16[512,1,128]{2,0,1:T(8,128)(2,1)S(1)}, u32[]{:S(2)}, u32[]{:S(2)}) collective-permute-start(bf16[512,1,128]{2,0,1:T(8,128)(2,1)S(1)} %fusion.40), channel_id=1, source_target_pairs={{128,0},{256,128},{384,256},{129,1},{257,129},{385,257},{130,2},{2... | collective-permute-start | bytes 393224 | tf_op jit(solution)/shard_map/ppermute | solution.py:14
  509.1 60.3 %all-to-all-start.10 = ((bf16[32,2,8192]{2,1,0:T(2,128)(2,1)}), bf16[32,2,8192]{2,1,0:T(2,128)(2,1)}, u32[]{:S(2)}, u32[]{:S(2)}) async-start(bf16[32,2,8192]{2,1,0:T(2,128)(2,1)} %reshape.439), calls=%async_computation.10 | async-start | bytes 2097152 | tf_op jit(solution)/shard_map/all_to_all | solution.py:150
  515.3 6.9 %collective-permute-start.2 = (bf16[512,1,128]{2,0,1:T(8,128)(2,1)S(1)}, bf16[512,1,128]{2,0,1:T(8,128)(2,1)S(1)}, u32[]{:S(2)}, u32[]{:S(2)}) collective-permute-start(bf16[512,1,128]{2,0,1:T(8,128)(2,1)S(1)} %fusion.39), channel_id=1, source_target_pairs={{128,0},{256,128},{384,256},{129,1},{257,129},{385,257},{130,2},{2... | collective-permute-start | bytes 393224 | tf_op jit(solution)/shard_map/ppermute | solution.py:14
  569.3 60.3 %all-to-all-start.9 = ((bf16[32,2,8192]{2,1,0:T(2,128)(2,1)}), bf16[32,2,8192]{2,1,0:T(2,128)(2,1)}, u32[]{:S(2)}, u32[]{:S(2)}) async-start(bf16[32,2,8192]{2,1,0:T(2,128)(2,1)} %reshape.437), calls=%async_computation.9 | async-start | bytes 2097152 | tf_op jit(solution)/shard_map/all_to_all | solution.py:147
where the time goes:
time: 641 us; the launch traced here: 637 us
  waiting for transfers between devices  301 us (47%)
  other arithmetic  80.2 us (13%)
  matrix products  78.5 us (12%)
  local copies, waits for them, and re-layouts  75.1 us (12%)
  starting transfers between devices  74.8 us (12%)
  blocking collectives  18.8 us (3%)
    all_to_all x1, waiting for transfers between devices, shards(): lax.all_to_all(key_rep, 'uly', split_axis=1, concat_axis=0, tiled=True)  53.9 us
    all_to_all x1, waiting for transfers between devices, shards(): lax.all_to_all(query_tok, 'uly', split_axis=1, concat_axis=0, tiled=True)  51.2 us
    all_to_all x1, waiting for transfers between devices, shards(): lax.all_to_all(value_rep, 'uly', split_axis=1, concat_axis=0, tiled=True)  51.2 us
    all_to_all x1, waiting for transfers between devices, shards(): lax.all_to_all(key_own.astype(jnp.bfloat16), 'uly', split_axis=0, concat_...  40.3 us
    all_to_all x1, waiting for transfers between devices, shards(): lax.all_to_all(grad_tok, 'uly', split_axis=1, concat_axis=0, tiled=True)  38.6 us
    unnamed x20, local copies, waits for them, and re-layouts  27.8 us
    convert_element_type x2, other arithmetic, shards(): value_own.astype(jnp.bfloat16)  27.1 us
    convert_element_type x2, other arithmetic, shards(): key_own.astype(jnp.bfloat16)  24.9 us
  transfers between devices with their start and end apart: 14, of which 14 were waited for; matrix products, arithmetic and copies ran while one was open for 14% of the time, Pallas kernels for 0%

commit v1 on v0

v1 whole, which is shorter than its diff:
```python
import functools
import math

import jax
import jax.numpy as jnp
from jax import lax
from jax.experimental import pallas as pl
from jax.experimental.pallas import tpu as pltpu
from jax.sharding import PartitionSpec as P

KVH = 4
RATIO = 8
HD = 128
GROUPS = 4
PIECE = 32
TILE = 128
ROW = 256
WIN = 640
MESH = pl.DeviceIdType.MESH
NT = (((1,), (1,)), ((), ()))
NN = (((1,), (0,)), ((), ()))
MASKED = -1e30


def kernel(
    n_rows, z_rows,
    assign_ref, seg_ref, q_ref, do_ref, k_ref, v_ref,
    gq_ref, gk_ref, gv_ref,
    kvs, qds, kvb, qdb, bias, kt, part, a_out, a_in, b_out, b_in, own, c_out, c_in,
    kv_send, kv_recv, qd_send, qd_recv, f_send, f_recv, r_send, r_recv,
):
    blk = lax.axis_index("blk")
    uly = lax.axis_index("uly")
    d = lax.axis_index("dp")
    xh = uly % 2
    z = uly // 2
    row = blk * z_rows + z
    me = xh * GROUPS + d

    def in_row(member):
        return (blk, z * 2 + member // GROUPS, member % GROUPS)

    def in_column(other):
        return (other // z_rows, (other % z_rows) * 2 + xh, d)

    up = in_column((row + 1) % n_rows)
    down = in_column((row + n_rows - 1) % n_rows)
    across = (blk, z * 2 + (1 - xh), d)

    barrier = pltpu.get_barrier_semaphore()
    partners = [in_row((me + i) % 8) for i in range(1, 8)] + [up, down]
    for partner in partners:
        pl.semaphore_signal(barrier, inc=1, device_id=partner, device_id_type=MESH)

    for g in range(GROUPS):
        a = assign_ref[g]
        for h in range(KVH):
            cols = slice(h * HD, (h + 1) * HD)
            kvs[g, h, 0] = k_ref[a, :, cols]
            kvs[g, h, 1] = v_ref[a, :, cols]
    for g in range(GROUPS):
        a = assign_ref[g]
        for h in range(KVH):
            for r in range(RATIO):
                cols = slice((h * RATIO + r) * HD, (h * RATIO + r + 1) * HD)
                qds[g, h, 0, r] = q_ref[a, :, cols]
                qds[g, h, 1, r] = do_ref[a, :, cols]

    here = pl.ds(pl.multiple_of(d * PIECE, PIECE), PIECE)
    mine = pl.ds(pl.multiple_of(2 * ROW + me * PIECE, PIECE), PIECE)
    for h in range(KVH):
        kvb[h, :, mine, :] = kvs[d, h]

    pl.semaphore_wait(barrier, len(partners))

    def kv_copy(h, i):
        member = (me + i) % 8
        return pltpu.make_async_remote_copy(
            src_ref=kvs.at[member % GROUPS, h],
            dst_ref=kvb.at[h, :, mine, :],
            send_sem=kv_send.at[h, i - 1],
            recv_sem=kv_recv.at[h, i - 1],
            device_id=in_row(member),
            device_id_type=MESH,
        )

    def qd_copy(h, i):
        g = (d + i) % GROUPS
        return pltpu.make_async_remote_copy(
            src_ref=qds.at[g, h],
            dst_ref=qdb.at[h, :, :, here, :],
            send_sem=qd_send.at[h, i - 1],
            recv_sem=qd_recv.at[h, i - 1],
            device_id=(blk, uly, g),
            device_id_type=MESH,
        )

    def forward(h, step):
        return pltpu.make_async_remote_copy(
            src_ref=kvb.at[h, :, pl.ds((2 - step) * ROW, ROW), :],
            dst_ref=kvb.at[h, :, pl.ds((1 - step) * ROW, ROW), :],
            send_sem=f_send.at[h, step],
            recv_sem=f_recv.at[h, step],
            device_id=up,
            device_id_type=MESH,
        )

    def back(h, step):
        src, dst, device = (
            (a_out, a_in, down), (b_out, b_in, down), (c_out, c_in, across)
        )[step]
        return pltpu.make_async_remote_copy(
            src_ref=src.at[h],
            dst_ref=dst.at[h],
            send_sem=r_send.at[h, step],
            recv_sem=r_recv.at[h, step],
            device_id=device,
            device_id_type=MESH,
        )

    for h in range(KVH):
        for i in range(1, 8):
            kv_copy(h, i).start()
    for h in range(KVH):
        for i in (2, 1, 3):
            qd_copy(h, i).start()

    for h in range(KVH):
        for t in range(2):
            qdb[h, t, :, here, :] = qds[d, h, t]

    tile = row * 2 + xh
    n_tiles = n_rows * 2
    mine_seq = assign_ref[d]
    chosen = lax.broadcasted_iota(jnp.int32, (GROUPS, TILE), 0) == mine_seq

    def segments(t):
        cols = pl.ds(pl.multiple_of(t * TILE, TILE), TILE)
        ids = jnp.where(chosen, seg_ref[:, cols], 0).astype(jnp.float32)
        return jnp.broadcast_to(jnp.sum(ids, axis=0, keepdims=True), (TILE, TILE))

    of_query = segments(tile)
    for i in range(5):
        t = tile - 4 + i
        of_key = jnp.transpose(segments((t + n_tiles) % n_tiles))
        allowed = of_key == of_query
        if i < 4:
            shut = jnp.where(t < 0, MASKED, 0.0).astype(jnp.float32)
            bias[i * TILE:(i + 1) * TILE, :] = jnp.where(allowed, shut, MASKED)
        else:
            key_at = lax.broadcasted_iota(jnp.int32, (TILE, TILE), 0)
            query_at = lax.broadcasted_iota(jnp.int32, (TILE, TILE), 1)
            bias[i * TILE:(i + 1) * TILE, :] = jnp.where(
                allowed & (key_at <= query_at), 0.0, MASKED
            )
    part[...] = jnp.zeros_like(part)

    def pass_row(h):
        for i in range(1, 8):
            kv_copy(h, i).wait_recv()
        forward(h, 0).start()

    def pass_on(h):
        forward(h, 0).wait_recv()
        forward(h, 1).start()

    window = pl.ds(pl.multiple_of(xh * TILE, TILE), WIN)
    scale = 1.0 / math.sqrt(HD)
    to_log2 = scale * math.log2(math.e)

    def compute(h):
        kt[...] = jnp.transpose(kvb[h, 0, window, :].astype(jnp.float32)).astype(jnp.bfloat16)

        def pair(j, _):
            key = kvb[h, 0, window, :]
            value = kvb[h, 1, window, :]
            query = qdb[h, 0, pl.ds(2 * j, 2)].reshape(2 * TILE, HD)
            grad = qdb[h, 1, pl.ds(2 * j, 2)].reshape(2 * TILE, HD)
            shut = bias[...]
            scores = lax.dot_general(key, query, NT, preferred_element_type=jnp.float32)
            scores = scores * to_log2 + jnp.concatenate([shut, shut], axis=1)
            weights = jnp.exp2(scores - jnp.max(scores, axis=0, keepdims=True))
            probs = weights * (1.0 / jnp.sum(weights, axis=0, keepdims=True))
            grad_probs = lax.dot_general(value, grad, NT, preferred_element_type=jnp.float32)
            delta = jnp.sum(probs * grad_probs, axis=0, keepdims=True)
            grad_scores = (scale * probs * (grad_probs - delta)).astype(jnp.bfloat16)
            part[h, 1, window, :] += lax.dot_general(
                probs.astype(jnp.bfloat16), grad, NN, preferred_element_type=jnp.float32
            )
            part[h, 0, window, :] += lax.dot_general(
                grad_scores, query, NN, preferred_element_type=jnp.float32
            )
            grad_query = lax.dot_general(
                kt[...], grad_scores, NN, preferred_element_type=jnp.float32
            )
            for r in range(2):
                cols = pl.ds(pl.multiple_of((h * RATIO + 2 * j + r) * HD, HD), HD)
                gq_ref[:, cols] = jnp.transpose(
                    grad_query[:, r * TILE:(r + 1) * TILE]
                ).astype(jnp.bfloat16)
            return 0

        lax.fori_loop(0, RATIO // 2, pair, 0)
        a_out[h] = part[h, :, :ROW, :].astype(jnp.bfloat16)

    def add_first(h):
        back(h, 0).wait_recv()
        total = part[h, :, ROW:2 * ROW, :] + a_in[h].astype(jnp.float32)
        b_out[h] = total.astype(jnp.bfloat16)

    def add_second(h):
        back(h, 1).wait_recv()
        keep = pl.ds(pl.multiple_of(xh * TILE, TILE), TILE)
        give = pl.ds(pl.multiple_of((1 - xh) * TILE, TILE), TILE)
        keep_part = pl.ds(pl.multiple_of(2 * ROW + xh * TILE, TILE), TILE)
        give_part = pl.ds(pl.multiple_of(2 * ROW + (1 - xh) * TILE, TILE), TILE)
        c_out[h] = (part[h, :, give_part, :] + b_in[h, :, give, :].astype(jnp.float32)).astype(jnp.bfloat16)
        own[h] = part[h, :, keep_part, :] + b_in[h, :, keep, :].astype(jnp.float32)

    def finish(h):
        back(h, 2).wait_recv()
        total = (own[h] + c_in[h].astype(jnp.float32)).astype(jnp.bfloat16)
        cols = slice(h * HD, (h + 1) * HD)
        gk_ref[:, cols] = total[0]
        gv_ref[:, cols] = total[1]

    passed = 0
    for h in range(KVH):
        pass_row(h)
        if h >= 1 and passed < min(2, KVH):
            pass_on(passed)
            passed += 1
    for h in range(KVH):
        for i in range(1, 4):
            qd_copy(h, i).wait_recv()
        if passed <= h:
            pass_on(passed)
            passed += 1
        forward(h, 1).wait_recv()
        compute(h)
        if passed < KVH:
            pass_on(passed)
            passed += 1
        back(h, 0).start()
        if h >= 1:
            add_first(h - 1)
            back(h - 1, 1).start()
        if h >= 2:
            add_second(h - 2)
            back(h - 2, 2).start()
        if h >= 3:
            finish(h - 3)
    for h in range(KVH, KVH + 3):
        if 0 <= h - 1 < KVH:
            add_first(h - 1)
            back(h - 1, 1).start()
        if 0 <= h - 2 < KVH:
            add_second(h - 2)
            back(h - 2, 2).start()
        if 0 <= h - 3 < KVH:
            finish(h - 3)

    for h in range(KVH):
        for i in range(1, 8):
            kv_copy(h, i).wait_send()
        for i in range(1, 4):
            qd_copy(h, i).wait_send()
        for step in range(2):
            forward(h, step).wait_send()
        for step in range(3):
            back(h, step).wait_send()


def shards(n_rows, z_rows, queries, keys, values, grad_out, segment_ids, assignment):
    bf16, f32 = jnp.bfloat16, jnp.float32
    vmem = pl.BlockSpec(memory_space=pltpu.VMEM)
    dma = pltpu.SemaphoreType.DMA
    gq, gk, gv = pl.pallas_call(
        functools.partial(kernel, n_rows, z_rows),
        out_shape=(
            jax.ShapeDtypeStruct((TILE, KVH * RATIO * HD), bf16),
            jax.ShapeDtypeStruct((TILE, KVH * HD), bf16),
            jax.ShapeDtypeStruct((TILE, KVH * HD), bf16),
        ),
        in_specs=[pl.BlockSpec(memory_space=pltpu.SMEM)] + [vmem] * 5,
        out_specs=(vmem, vmem, vmem),
        scratch_shapes=[
            pltpu.VMEM((GROUPS, KVH, 2, PIECE, HD), bf16),
            pltpu.VMEM((GROUPS, KVH, 2, RATIO, PIECE, HD), bf16),
            pltpu.VMEM((KVH, 2, 3 * ROW, HD), bf16),
            pltpu.VMEM((KVH, 2, RATIO, TILE, HD), bf16),
            pltpu.VMEM((WIN, TILE), f32),
            pltpu.VMEM((HD, WIN), bf16),
            pltpu.VMEM((KVH, 2, 3 * ROW, HD), f32),
            pltpu.VMEM((KVH, 2, ROW, HD), bf16),
            pltpu.VMEM((KVH, 2, ROW, HD), bf16),
            pltpu.VMEM((KVH, 2, ROW, HD), bf16),
            pltpu.VMEM((KVH, 2, ROW, HD), bf16),
            pltpu.VMEM((KVH, 2, TILE, HD), f32),
            pltpu.VMEM((KVH, 2, TILE, HD), bf16),
            pltpu.VMEM((KVH, 2, TILE, HD), bf16),
            dma((KVH, 7)), dma((KVH, 7)),
            dma((KVH, 3)), dma((KVH, 3)),
            dma((KVH, 2)), dma((KVH, 2)),
            dma((KVH, 3)), dma((KVH, 3)),
        ],
        compiler_params=pltpu.CompilerParams(
            collective_id=0, has_side_effects=True, vmem_limit_bytes=60 * 1024 * 1024
        ),
        name="attention_backward",
    )(assignment, segment_ids, queries, grad_out, keys, values)
    return gq.reshape(1, TILE, KVH * RATIO, HD), gk[None], gv[None]


def solution(mesh):
    z_rows = mesh.shape["uly"] // 2
    n_rows = mesh.shape["blk"] * z_rows
    tokens = P(None, ("blk", "uly", "dp"), None)
    return jax.shard_map(
        functools.partial(shards, n_rows, z_rows),
        mesh=mesh,
        in_specs=(tokens, tokens, tokens, tokens, P(), P()),
        out_specs=(
            P("dp", ("blk", "uly"), None, None),
            P("dp", ("blk", "uly"), None),
            P("dp", ("blk", "uly"), None),
        ),
        check_vma=False,
    )
```

time: 641 us -> 71.9 us (0.11)
  the two profiles are of different devices: /device:TPU:52 before, /device:TPU:4 now
where the time goes in v1:
time: 71.9 us; the launch traced here: 71.7 us
  Pallas kernels  67 us (93%)
  local copies, waits for them, and re-layouts  4.07 us (6%)
    pallas_call x1, Pallas kernels, shards(): pl.pallas_call(functools.partial(kernel, n_rows, z_rows), out_shape=(jax....  67 us
    unnamed x7, local copies, waits for them, and re-layouts  4.07 us

profile of v1, /device:TPU:4, one launch (start us, length us, event | category | flops | bytes accessed | tf_op | source)
XLA Modules:
  0.0 71.7 jit_solution(13438366909380426253)
XLA Ops:
  0.6 67.0 %attention_backward.1 = (bf16[128,4096]{1,0:T(8,128)(2,1)}, bf16[128,512]{1,0:T(8,128)(2,1)}, bf16[128,512]{1,0:T(8,128)(2,1)}) custom-call(s32[4]{0:T(128)} %assign_ref.1, s32[4,16384]{1,0:T(4,128)} %seg_ref.1, bf16[4,32,4096]{2,1,0:T(8,128)(2,1)} %q_ref.1, bf16[4,32,4096]{2,1,0:T(8,128)(2,1)} %do_ref.1, bf16[4,32,512]{2,1,0:T(8,128)(2,1)} %k_ref.1, ...), custom_call_target="tpu_custom_call" | custom-call | tf_op jit(solution)/shard_map/attention_backward/pallas_call | solution.py:278
  67.7 0.0 copy-start.1
  67.7 2.5 %copy.9 = bf16[16,8,32,128]{3,2,1,0:T(8,128)(2,1)} copy(bf16[16,8,32,128]{3,1,2,0:T(8,128)(2,1)} %bitcast.6) | data formatting | bytes 2097152
  70.1 0.0 copy-done.1
  70.1 0.0 copy-start
  70.1 0.7 copy.12
  70.8 0.3 copy-done
  71.1 0.7 copy.13
Async XLA Ops:
  67.7 2.5 %copy-start.1 = (bf16[128,512]{1,0:T(8,128)(2,1)S(1)}, bf16[128,512]{1,0:T(8,128)(2,1)}, u32[]{:S(2)}) copy-start(bf16[128,512]{1,0:T(8,128)(2,1)} %get-tuple-element.7) | copy-start | bytes 393220
  70.1 1.0 %copy-start = (bf16[128,512]{1,0:T(8,128)(2,1)S(1)}, bf16[128,512]{1,0:T(8,128)(2,1)}, u32[]{:S(2)}) copy-start(bf16[128,512]{1,0:T(8,128)(2,1)} %get-tuple-element.8) | copy-start | bytes 393220

commit v2 on v1

v2 whole, which is shorter than its diff:
```python
import functools
import math

import jax
import jax.numpy as jnp
from jax import lax
from jax.experimental import pallas as pl
from jax.experimental.pallas import tpu as pltpu
from jax.sharding import PartitionSpec as P

KVH = 4
RATIO = 8
HD = 128
GROUPS = 4
PIECE = 32
TILE = 128
ROW = 256
WIN = 640
MESH = pl.DeviceIdType.MESH
NT = (((1,), (1,)), ((), ()))
NN = (((1,), (0,)), ((), ()))
MASKED = -1e30


def kernel(
    n_rows, z_rows,
    assign_hbm, seg_hbm, q_hbm, do_hbm, k_hbm, v_hbm,
    gq_ref, gk_ref, gv_ref,
    assign_ref, seg_ref, k_ref, v_ref, in_sem, kvs, qds, kvb, qdb, bias, kt, gq_part, part, a_out, a_in, b_out, b_in, own, c_out, c_in,
    kv_send, kv_recv, qd_send, qd_recv, f_send, f_recv, r_send, r_recv, x_send, x_recv, g_send, g_recv,
    *fetched,
):
    blk = lax.axis_index("blk")
    uly = lax.axis_index("uly")
    d = lax.axis_index("dp")
    xh = uly % 2
    z = uly // 2
    row = blk * z_rows + z
    me = xh * GROUPS + d

    def in_row(member):
        return (blk, z * 2 + member // GROUPS, member % GROUPS)

    def in_column(other):
        return (other // z_rows, (other % z_rows) * 2 + xh, d)

    up = in_column((row + 1) % n_rows)
    down = in_column((row + n_rows - 1) % n_rows)
    across = (blk, z * 2 + (1 - xh), d)
    up_across = (up[0], up[1] + 1 - 2 * xh, d)
    down_across = (down[0], down[1] + 1 - 2 * xh, d)

    def fetch_keys():
        return [
            pltpu.make_async_copy(k_hbm, k_ref, in_sem.at[0]),
            pltpu.make_async_copy(v_hbm, v_ref, in_sem.at[1]),
        ]

    def fetch_queries(h):
        cols = pl.ds(h * RATIO * HD, RATIO * HD)
        return [
            pltpu.make_async_copy(src.at[:, :, cols], fetched[2 * h + i], in_sem.at[3 + 2 * h + i])
            for i, src in enumerate((q_hbm, do_hbm))
        ]

    fetch_assignment = pltpu.make_async_copy(assign_hbm, assign_ref, in_sem.at[3 + 2 * KVH])
    fetch_assignment.start()
    fetch_segments = pltpu.make_async_copy(seg_hbm, seg_ref, in_sem.at[2])
    for copy in fetch_keys():
        copy.start()
    for h in range(KVH):
        for copy in fetch_queries(h):
            copy.start()
    fetch_segments.start()

    barrier = pltpu.get_barrier_semaphore()
    partners = [in_row((me + i) % 8) for i in range(1, 8)] + [up, down, up_across, down_across]
    for partner in partners:
        pl.semaphore_signal(barrier, inc=1, device_id=partner, device_id_type=MESH)

    def stage_keys(h):
        cols = slice(h * HD, (h + 1) * HD)
        for g in range(GROUPS):
            a = assign_ref[g]
            kvs[g, h, 0] = k_ref[a, :, cols]
            kvs[g, h, 1] = v_ref[a, :, cols]

    def stage_queries(h):
        for copy in fetch_queries(h):
            copy.wait()
        for g in range(GROUPS):
            a = assign_ref[g]
            for r in range(RATIO):
                cols = slice(r * HD, (r + 1) * HD)
                qds[g, h, 0, r] = fetched[2 * h][a, :, cols]
                qds[g, h, 1, r] = fetched[2 * h + 1][a, :, cols]

    fetch_assignment.wait()
    for copy in fetch_keys():
        copy.wait()
    for h in range(KVH):
        stage_keys(h)
    stage_queries(0)

    here = pl.ds(pl.multiple_of(d * PIECE, PIECE), PIECE)
    mine = pl.ds(pl.multiple_of(2 * ROW + me * PIECE, PIECE), PIECE)
    for h in range(KVH):
        kvb[h, :, mine, :] = kvs[d, h]

    pl.semaphore_wait(barrier, len(partners))

    def kv_copy(h, i):
        member = (me + i) % 8
        return pltpu.make_async_remote_copy(
            src_ref=kvs.at[member % GROUPS, h],
            dst_ref=kvb.at[h, :, mine, :],
            send_sem=kv_send.at[h, i - 1],
            recv_sem=kv_recv.at[h, i - 1],
            device_id=in_row(member),
            device_id_type=MESH,
        )

    def qd_copy(h, j, i):
        g = (d + i) % GROUPS
        heads = pl.ds(2 * j, 2)
        return pltpu.make_async_remote_copy(
            src_ref=qds.at[g, h, :, heads],
            dst_ref=qdb.at[h, :, heads, here, :],
            send_sem=qd_send.at[h, j, i - 1],
            recv_sem=qd_recv.at[h, j, i - 1],
            device_id=(blk, uly, g),
            device_id_type=MESH,
        )

    def forward(h, step):
        return pltpu.make_async_remote_copy(
            src_ref=kvb.at[h, :, pl.ds((2 - step) * ROW, ROW), :],
            dst_ref=kvb.at[h, :, pl.ds((1 - step) * ROW, ROW), :],
            send_sem=f_send.at[h, step],
            recv_sem=f_recv.at[h, step],
            device_id=up,
            device_id_type=MESH,
        )

    keep = pl.ds(pl.multiple_of(xh * TILE, TILE), TILE)
    give = pl.ds(pl.multiple_of((1 - xh) * TILE, TILE), TILE)

    def direct(h):
        return h == KVH - 1

    def back(h, step, t):
        src, dst, device = ((a_out, a_in, down), (b_out, b_in, down))[step]
        rows = (give, keep)[t]
        if direct(h) and step == 1 and t == 0:
            return pltpu.make_async_remote_copy(
                src_ref=b_out.at[h, :, give, :],
                dst_ref=b_in.at[h, :, keep, :],
                send_sem=g_send,
                recv_sem=g_recv,
                device_id=down_across,
                device_id_type=MESH,
            )
        return pltpu.make_async_remote_copy(
            src_ref=src.at[h, :, rows, :],
            dst_ref=dst.at[h, :, rows, :],
            send_sem=r_send.at[h, step, t],
            recv_sem=r_recv.at[h, step, t],
            device_id=device,
            device_id_type=MESH,
        )

    def cross(h):
        return pltpu.make_async_remote_copy(
            src_ref=c_out.at[h],
            dst_ref=c_in.at[h],
            send_sem=x_send.at[h],
            recv_sem=x_recv.at[h],
            device_id=across,
            device_id_type=MESH,
        )

    def send_keys(h):
        for i in range(1, 8):
            kv_copy(h, i).start()

    def send_queries(h):
        for j in range(RATIO // 2):
            for i in (2, 1, 3):
                qd_copy(h, j, i).start()

    send_keys(0)
    send_keys(1)
    stage_queries(1)
    send_queries(0)
    send_keys(2)
    send_keys(3)
    stage_queries(2)
    send_queries(1)
    stage_queries(3)
    send_queries(2)
    send_queries(3)

    for h in range(KVH):
        for t in range(2):
            qdb[h, t, :, here, :] = qds[d, h, t]

    fetch_segments.wait()
    tile = row * 2 + xh
    n_tiles = n_rows * 2
    mine_seq = assign_ref[d]
    chosen = lax.broadcasted_iota(jnp.int32, (GROUPS, TILE), 0) == mine_seq

    def segments(t):
        cols = pl.ds(pl.multiple_of(t * TILE, TILE), TILE)
        ids = jnp.where(chosen, seg_ref[:, cols], 0).astype(jnp.float32)
        return jnp.broadcast_to(jnp.sum(ids, axis=0, keepdims=True), (TILE, TILE))

    of_query = segments(tile)
    for i in range(5):
        t = tile - 4 + i
        of_key = jnp.transpose(segments((t + n_tiles) % n_tiles))
        allowed = of_key == of_query
        if i < 4:
            shut = jnp.where(t < 0, MASKED, 0.0).astype(jnp.float32)
            bias[i * TILE:(i + 1) * TILE, :] = jnp.where(allowed, shut, MASKED)
        else:
            key_at = lax.broadcasted_iota(jnp.int32, (TILE, TILE), 0)
            query_at = lax.broadcasted_iota(jnp.int32, (TILE, TILE), 1)
            bias[i * TILE:(i + 1) * TILE, :] = jnp.where(
                allowed & (key_at <= query_at), 0.0, MASKED
            )
    part[...] = jnp.zeros_like(part)

    def pass_row(h):
        for i in range(1, 8):
            kv_copy(h, i).wait_recv()
        forward(h, 0).start()

    def pass_on(h):
        forward(h, 0).wait_recv()
        forward(h, 1).start()

    window = pl.ds(pl.multiple_of(xh * TILE, TILE), WIN)
    scale = 1.0 / math.sqrt(HD)
    to_log2 = scale * math.log2(math.e)

    def compute(h, first, last):
        if first == 0:
            forward(h, 1).wait_recv()
            kt[...] = jnp.transpose(
                kvb[h, 0, window, :].astype(jnp.float32)
            ).astype(jnp.bfloat16)

        def pair(j, _):
            for i in range(1, 4):
                qd_copy(h, j, i).wait_recv()
            key = kvb[h, 0, window, :]
            value = kvb[h, 1, window, :]
            query = qdb[h, 0, pl.ds(2 * j, 2)].reshape(2 * TILE, HD)
            grad = qdb[h, 1, pl.ds(2 * j, 2)].reshape(2 * TILE, HD)
            shut = bias[...]
            scores = lax.dot_general(key, query, NT, preferred_element_type=jnp.float32)
            scores = scores * to_log2 + jnp.concatenate([shut, shut], axis=1)
            weights = jnp.exp2(scores - jnp.max(scores, axis=0, keepdims=True))
            probs = weights * (1.0 / jnp.sum(weights, axis=0, keepdims=True))
            grad_probs = lax.dot_general(value, grad, NT, preferred_element_type=jnp.float32)
            delta = jnp.sum(probs * grad_probs, axis=0, keepdims=True)
            grad_scores = (scale * probs * (grad_probs - delta)).astype(jnp.bfloat16)
            part[h, 1, window, :] += lax.dot_general(
                probs.astype(jnp.bfloat16), grad, NN, preferred_element_type=jnp.float32
            )
            part[h, 0, window, :] += lax.dot_general(
                grad_scores, query, NN, preferred_element_type=jnp.float32
            )
            grad_query = lax.dot_general(
                kt[...], grad_scores, NN, preferred_element_type=jnp.float32
            )
            for r in range(2):
                head = h * RATIO + 2 * j + r
                gq_part[pl.ds(head, TILE, stride=KVH * RATIO), :] = jnp.transpose(
                    grad_query[:, r * TILE:(r + 1) * TILE]
                )
            return 0

        lax.fori_loop(first, last, pair, 0)

    keep_at = pl.ds(pl.multiple_of(2 * ROW + xh * TILE, TILE), TILE)
    give_at = pl.ds(pl.multiple_of(2 * ROW + (1 - xh) * TILE, TILE), TILE)

    def start_return(h):
        a_out[h] = part[h, :, :ROW, :].astype(jnp.bfloat16)
        if direct(h):
            c_out[h] = part[h, :, give_at, :].astype(jnp.bfloat16)
        for t in range(2):
            back(h, 0, t).start()
        if direct(h):
            cross(h).start()

    def add_first(h):
        for t, rows in enumerate((give, keep)):
            back(h, 0, t).wait_recv()
            offset = (1 - xh) if t == 0 else xh
            at = pl.ds(pl.multiple_of(ROW + offset * TILE, TILE), TILE)
            total = part[h, :, at, :] + a_in[h, :, rows, :].astype(jnp.float32)
            b_out[h, :, rows, :] = total.astype(jnp.bfloat16)
            back(h, 1, t).start()

    def add_second(h):
        if not direct(h):
            back(h, 1, 0).wait_recv()
            total = part[h, :, give_at, :] + b_in[h, :, give, :].astype(jnp.float32)
            c_out[h] = total.astype(jnp.bfloat16)
            cross(h).start()
        back(h, 1, 1).wait_recv()
        own[h] = part[h, :, keep_at, :] + b_in[h, :, keep, :].astype(jnp.float32)

    def finish(h):
        cross(h).wait_recv()
        total = own[h] + c_in[h].astype(jnp.float32)
        if direct(h):
            back(h, 1, 0).wait_recv()
            total += b_in[h, :, give, :].astype(jnp.float32)
        total = total.astype(jnp.bfloat16)
        cols = slice(h * HD, (h + 1) * HD)
        gk_ref[:, cols] = total[0]
        gv_ref[:, cols] = total[1]

    def write_queries(h):
        heads = gq_part[...].reshape(TILE, KVH * RATIO, HD)
        part_of = slice((h - 1) * RATIO, (h + 1) * RATIO)
        gq_ref[0, :, part_of, :] = heads[:, part_of, :].astype(jnp.bfloat16)

    pairs = RATIO // 2
    pass_row(0)
    pass_row(1)
    pass_on(0)
    pass_on(1)
    pass_row(2)
    compute(0,0,1)
    pass_row(3)
    compute(0,1,pairs)
    start_return(0)
    compute(1,0,2)
    pass_on(2)
    compute(1,2,pairs)
    start_return(1)
    add_first(0)
    pass_on(3)
    write_queries(1)
    compute(2,0,2)
    add_first(1)
    add_second(0)
    compute(2,2,pairs)
    start_return(2)
    finish(0)
    compute(3,0,2)
    add_second(1)
    compute(3,2,3)
    add_first(2)
    compute(3,3,pairs)
    start_return(3)
    write_queries(3)
    finish(1)
    add_first(3)
    add_second(2)
    finish(2)
    add_second(3)
    finish(3)

    for h in range(KVH):
        for i in range(1, 8):
            kv_copy(h, i).wait_send()
        for j in range(RATIO // 2):
            for i in range(1, 4):
                qd_copy(h, j, i).wait_send()
        for step in range(2):
            forward(h, step).wait_send()
            for t in range(2):
                back(h, step, t).wait_send()
        cross(h).wait_send()


def write_out(gq_ref, gk_ref, gv_ref, gq_out, gk_out, gv_out, sem):
    copies = [
        pltpu.make_async_copy(gq_ref, gq_out, sem.at[0]),
        pltpu.make_async_copy(gk_ref, gk_out.at[0], sem.at[1]),
        pltpu.make_async_copy(gv_ref, gv_out.at[0], sem.at[2]),
    ]
    for copy in copies:
        copy.start()
    for copy in copies:
        copy.wait()


def shards(n_rows, z_rows, queries, keys, values, grad_out, segment_ids, assignment):
    bf16, f32 = jnp.bfloat16, jnp.float32
    vmem = pl.BlockSpec(memory_space=pltpu.VMEM)
    dma = pltpu.SemaphoreType.DMA
    gq, gk, gv = pl.pallas_call(
        functools.partial(kernel, n_rows, z_rows),
        out_shape=(
            jax.ShapeDtypeStruct((1, TILE, KVH * RATIO, HD), bf16),
            jax.ShapeDtypeStruct((TILE, KVH * HD), bf16),
            jax.ShapeDtypeStruct((TILE, KVH * HD), bf16),
        ),
        in_specs=[pl.BlockSpec(memory_space=pltpu.HBM)] * 6,
        out_specs=(vmem, vmem, vmem),
        scratch_shapes=[
            pltpu.SMEM((GROUPS,), jnp.int32),
            pltpu.VMEM(segment_ids.shape, jnp.int32),
            pltpu.VMEM(keys.shape, bf16),
            pltpu.VMEM(keys.shape, bf16),
            dma((4 + 2 * KVH,)),
            pltpu.VMEM((GROUPS, KVH, 2, PIECE, HD), bf16),
            pltpu.VMEM((GROUPS, KVH, 2, RATIO, PIECE, HD), bf16),
            pltpu.VMEM((KVH, 2, 3 * ROW, HD), bf16),
            pltpu.VMEM((KVH, 2, RATIO, TILE, HD), bf16),
            pltpu.VMEM((WIN, TILE), f32),
            pltpu.VMEM((HD, WIN), bf16),
            pltpu.VMEM((TILE * KVH * RATIO, HD), f32),
            pltpu.VMEM((KVH, 2, 3 * ROW, HD), f32),
            pltpu.VMEM((KVH, 2, ROW, HD), bf16),
            pltpu.VMEM((KVH, 2, ROW, HD), bf16),
            pltpu.VMEM((KVH, 2, ROW, HD), bf16),
            pltpu.VMEM((KVH, 2, ROW, HD), bf16),
            pltpu.VMEM((KVH, 2, TILE, HD), f32),
            pltpu.VMEM((KVH, 2, TILE, HD), bf16),
            pltpu.VMEM((KVH, 2, TILE, HD), bf16),
            dma((KVH, 7)), dma((KVH, 7)),
            dma((KVH, RATIO // 2, 3)), dma((KVH, RATIO // 2, 3)),
            dma((KVH, 2)), dma((KVH, 2)),
            dma((KVH, 2, 2)), dma((KVH, 2, 2)),
            dma((KVH,)), dma((KVH,)), dma(()), dma(()),
        ]
        + [pltpu.VMEM((GROUPS, PIECE, RATIO * HD), bf16)] * (2 * KVH),
        compiler_params=pltpu.CompilerParams(
            collective_id=0, has_side_effects=True, vmem_limit_bytes=32 * 1024 * 1024
        ),
        name="attention_backward",
    )(
        *(
            pltpu.with_memory_space_constraint(array, pltpu.HBM)
            for array in (assignment, segment_ids, queries, grad_out, keys, values)
        )
    )
    return pl.pallas_call(
        write_out,
        out_shape=(
            jax.ShapeDtypeStruct(gq.shape, bf16),
            jax.ShapeDtypeStruct((1,) + gk.shape, bf16),
            jax.ShapeDtypeStruct((1,) + gv.shape, bf16),
        ),
        in_specs=[vmem] * 3,
        out_specs=[pl.BlockSpec(memory_space=pl.ANY)] * 3,
        scratch_shapes=[dma((3,))],
        compiler_params=pltpu.CompilerParams(vmem_limit_bytes=4 * 1024 * 1024),
        name="write_out",
    )(gq, gk, gv)


def solution(mesh):
    z_rows = mesh.shape["uly"] // 2
    n_rows = mesh.shape["blk"] * z_rows
    tokens = P(None, ("blk", "uly", "dp"), None)
    return jax.shard_map(
        functools.partial(shards, n_rows, z_rows),
        mesh=mesh,
        in_specs=(tokens, tokens, tokens, tokens, P(), P()),
        out_specs=(
            P("dp", ("blk", "uly"), None, None),
            P("dp", ("blk", "uly"), None),
            P("dp", ("blk", "uly"), None),
        ),
        check_vma=False,
    )
```

time: 71.9 us -> 65.9 us (0.917)
  the two profiles are of different devices: /device:TPU:4 before, /device:TPU:2 now
where the time goes in v2:
time: 65.9 us; the launch traced here: 65.8 us
  Pallas kernels  65.1 us (99%)
    pallas_call x1, Pallas kernels, shards(): pl.pallas_call(functools.partial(kernel, n_rows, z_rows), out_shape=(jax....  64.1 us

profile of v2, /device:TPU:2, one launch (start us, length us, event | category | flops | bytes accessed | tf_op | source)
XLA Modules:
  0.0 65.8 jit_solution(1646406370943463426)
XLA Ops:
  0.6 64.1 %attention_backward.1 = (bf16[1,128,32,128]{3,2,1,0:T(8,128)(2,1)S(1)}, bf16[128,512]{1,0:T(8,128)(2,1)S(1)}, bf16[128,512]{1,0:T(8,128)(2,1)S(1)}) custom-call(s32[4]{0:T(128)} %assign_hbm.1, s32[4,16384]{1,0:T(4,128)} %seg_hbm.1, bf16[4,32,4096]{2,1,0:T(8,128)(2,1)} %q_hbm.1, bf16[4,32,4096]{2,1,0:T(8,128)(2,1)} %do_hbm.1, bf16[4,32,512]{2,1,0:T(8,128)(2,1)} %k_hbm.1, ...), custom_call_target="tpu_custom_call" | custom-call | tf_op jit(solution)/shard_map/attention_backward/pallas_call | solution.py:399
  64.7 1.1 %write_out.1 = (bf16[1,128,32,128]{3,2,1,0:T(8,128)(2,1)}, bf16[1,128,512]{2,1,0:T(8,128)(2,1)}, bf16[1,128,512]{2,1,0:T(8,128)(2,1)}) custom-call(bf16[1,128,32,128]{3,2,1,0:T(8,128)(2,1)S(1)} %get-tuple-element.6.gq_ref, bf16[128,512]{1,0:T(8,128)(2,1)S(1)} %get-tuple-element.7.gk_ref, bf16[128,512]{1,0:T(8,128)(2,1)S(1)} %get-tuple-element.8.gv_ref), custom_call_target="tpu_custom_call" | custom-call | tf_op jit(solution)/shard_map/write_out/pallas_call | solution.py:446
